TPU v7x, 256 devices: a whole 4x4x8 slice. The times are simulated.
256 devices in a mesh: row: 64 (over y, z, core), col: 4 (over x).
Axes of the slice: x: 4, y: 4, z: 8, core: 2. Of those that a mesh axis runs over, the one named last changes fastest.
Arguments:
- leaf_grad: bfloat16 [256, 32, 1024], P('row', None, 'col'), may hold values from -6 to 6
- leaf_inv: bfloat16 [256, 1024, 1024], P('row', 'col'), as said below
- leaf_cpl: bfloat16 [256, 1024, 512], P('row', 'col'), may hold values from -0.046875 to 0.046875
- leaf_size: int32 [256], P('row'), may hold values from 256 to 1024, as said below
- leaf_parent: int32 [256], P('row'), may hold values from 0 to 3
- leaf_map: int32 [256, 512], P('row'), may hold values from 0 to 2047
- mid_grad: bfloat16 [32, 4, 2048], P(None, 'col', 'row'), may hold values from -6 to 6
- mid_inv: bfloat16 [4, 2048, 2048], P('col', 'row'), as said below
- mid_cpl: bfloat16 [4, 2048, 512], P('col', 'row'), may hold values from -0.125 to 0.125
- mid_map: int32 [4, 512], replicated, may hold values from 0 to 2047
- root_grad: bfloat16 [32, 2048], P(None, 'row'), may hold values from -6 to 6
- root_inv: bfloat16 [2048, 2048], P('row'), as said below
Outputs:
- leaf_x: float32 [256, 32, 1024], P('row', None, 'col')
- mid_x: float32 [32, 4, 2048], P(None, 'col', 'row')
- root_x: float32 [32, 2048], P(None, 'row')
Inputs may be any that keep to these rules, and one draw needn't show every extreme that they name: `leaf_size`: some leaf in every draw has 1024 live pivot columns. `leaf_map`: columns may repeat. `mid_map`: columns may repeat. `leaf_inv`: upper triangular; diagonal entries between 1 and 1.25, entries above the diagonal of scale 1024 ** -0.5. `mid_inv`: each front's block is upper triangular; diagonal entries between 1 and 1.25, entries above the diagonal of scale 2048 ** -0.5. `root_inv`: upper triangular; diagonal entries between 1 and 1.25, entries above the diagonal of scale 2048 ** -0.5.
All inputs are finite; a program needn't handle non-finite values.
Results may differ from a plain program's by a relative error of at most 0.012.
Values may be sent and summed in bfloat16 or wider, within the bound.
No kernel may reach another device: no remote copies, remote signals or barrier semaphores. Data moves between devices by JAX's collectives and lax.ppermute only.
A program may use at most 64 MiB of HBM per device.

v0:
```python
import jax
import jax.numpy as jnp
from jax import lax
from jax.sharding import PartitionSpec as P


def body(
    leaf_grad,
    leaf_inv,
    leaf_cpl,
    leaf_size,
    leaf_parent,
    leaf_map,
    mid_grad,
    mid_inv,
    mid_cpl,
    mid_map,
    root_grad,
    root_inv,
):
    ncolumns = lax.axis_size("col")
    row_id = lax.axis_index("row")
    col_id = lax.axis_index("col")
    nleaves = leaf_inv.shape[0]
    share_rows = leaf_inv.shape[1]
    nrhs = leaf_grad.shape[1]
    front = mid_inv.shape[2]
    mid_rows = mid_inv.shape[1]
    nmiddle = mid_map.shape[0]
    root_order = root_inv.shape[1]
    root_rows = root_inv.shape[0]
    inv_block = mid_inv[0]
    cpl_block = mid_cpl[0]
    first_cols = col_id * share_rows + lax.iota(jnp.int32, share_rows)
    live = (first_cols[None, :] < leaf_size[:, None])[:, None, :]
    partial_value = jnp.einsum(
        "lkp,lpq->lkq", leaf_grad, leaf_inv, preferred_element_type=jnp.float32
    )
    leaf_y = jnp.where(
        live, lax.psum_scatter(partial_value, "col", scatter_dimension=2, tiled=True), 0.0
    )
    leaf_yb = leaf_y.astype(jnp.bfloat16)
    shares = jnp.einsum("lkp,lpc->klc", leaf_yb, leaf_cpl, preferred_element_type=jnp.float32)
    placed_cols = (
        leaf_map // mid_rows * ncolumns + leaf_parent[:, None]
    ) * mid_rows + leaf_map % mid_rows
    targets = placed_cols.reshape(-1)
    spread = (
        jnp.zeros((nrhs, nmiddle * front), jnp.float32).at[:, targets].add(shares.reshape(nrhs, -1))
    )
    arrived = lax.psum_scatter(spread, ("row", "col"), scatter_dimension=1, tiled=True)
    mid_hb = (mid_grad[:, 0, :].astype(jnp.float32) - arrived).astype(jnp.bfloat16)
    mid_part = jnp.dot(mid_hb, inv_block, preferred_element_type=jnp.float32)
    mid_y = lax.psum_scatter(mid_part, "row", scatter_dimension=1, tiled=True)
    mid_yb = mid_y.astype(jnp.bfloat16)
    mid_share = jnp.dot(mid_yb, cpl_block, preferred_element_type=jnp.float32)
    root_cols = lax.dynamic_index_in_dim(mid_map, col_id, 0, keepdims=False)
    root_term = jnp.zeros((nrhs, root_order), jnp.float32).at[:, root_cols].add(mid_share)
    root_total = lax.psum(root_term, ("row", "col"))
    root_slice = lax.dynamic_slice_in_dim(root_total, row_id * root_rows, root_rows, 1)
    root_hb = (root_grad.astype(jnp.float32) - root_slice).astype(jnp.bfloat16)
    root_y = lax.psum(jnp.dot(root_hb, root_inv, preferred_element_type=jnp.float32), "row")
    root_yb = root_y.astype(jnp.bfloat16)
    root_x = jnp.einsum("kq,pq->kp", root_yb, root_inv, preferred_element_type=jnp.float32)
    root_all = lax.all_gather(root_x.astype(jnp.bfloat16), "row", axis=1, tiled=True)
    coupled = root_all[:, root_cols]
    mid_wb = (
        mid_y - jnp.einsum("kc,bc->kb", coupled, cpl_block, preferred_element_type=jnp.float32)
    ).astype(jnp.bfloat16)
    full_w = lax.all_gather(mid_wb, "row", axis=1, tiled=True)
    mid_x = jnp.einsum("kq,bq->kb", full_w, inv_block, preferred_element_type=jnp.float32)
    all_mid = lax.all_gather(mid_x.astype(jnp.bfloat16), ("row", "col"), axis=1, tiled=True)
    picked = all_mid[:, targets].reshape(nrhs, nleaves, -1)
    leaf_w = leaf_y - jnp.einsum(
        "klc,lpc->lkp", picked, leaf_cpl, preferred_element_type=jnp.float32
    )
    leaf_wb = jnp.where(live, leaf_w, 0.0).astype(jnp.bfloat16)
    leaf_x = jnp.einsum(
        "lkq,lpq->lkp",
        lax.all_gather(leaf_wb, "col", axis=2, tiled=True),
        leaf_inv,
        preferred_element_type=jnp.float32,
    )
    return (leaf_x, mid_x[:, None, :], root_x)


def solution(mesh):
    placed = (
        P("row", None, "col"),
        P("row", "col", None),
        P("row", "col", None),
        P("row"),
        P("row"),
        P("row", None),
        P(None, "col", "row"),
        P("col", "row", None),
        P("col", "row", None),
        P(),
        P(None, "row"),
        P("row", None),
    )
    return jax.shard_map(
        body,
        mesh=mesh,
        in_specs=placed,
        out_specs=(P("row", None, "col"), P(None, "col", "row"), P(None, "row")),
        check_vma=False,
    )
```

profile of v0, /device:TPU:8, one launch (start us, length us, event | category | flops | bytes accessed | tf_op | source)
XLA Modules:
  0.0 2242.4 jit_solution(18431036264109343897)
XLA Ops:
  7.3 1.5 copy-done
  8.8 2.1 fusion.32
  11.2 26.7 %reduce-scatter.6.cloned.1.call-done = f32[4,32,256]{2,1,0:T(8,128)} async-done(((f32[4,32,1024]{2,1,0:T(8,128)}), f32[4,32,256]{2,1,0:T(8,128)}) %reduce-scatter.6.cloned.1.call-update) | async-done | bytes 131088 | tf_op jit(solution)/shard_map/reduce_scatter | solution.py:40
  37.9 1.2 convolution_bitcast_fusion.1
  39.1 1.3 copy.29
  40.4 14.0 scatter_custom_fusion
  55.2 1119.9 %reduce-scatter.8.cloned.1.call-done = f32[32,32]{0,1:T(8,128)} async-done(((f32[32,8192]{0,1:T(8,128)}), f32[32,32]{0,1:T(8,128)}) %reduce-scatter.8.cloned.1.call-update) | async-done | bytes 4112 | tf_op jit(solution)/shard_map/reduce_scatter | solution.py:51
  1175.1 2.0 convolution_bitcast_fusion
  1178.0 286.1 %reduce-scatter.10.cloned.1.call-done = f32[32,32]{1,0:T(8,128)} async-done(((f32[2048,32]{1,0:T(8,128)}), f32[32,32]{1,0:T(8,128)}) %reduce-scatter.10.cloned.1.call-update) | async-done | bytes 4112
  1465.8 3.6 scatter_custom_fusion.1
  1471.3 254.1 %all-reduce.3.cloned.1.call-done = f32[32,2048]{0,1:T(8,128)} async-done(((f32[32,2048]{0,1:T(8,128)}), f32[32,2048]{0,1:T(8,128)}) %all-reduce.3.cloned.1.call-update) | async-done | bytes 262160 | tf_op jit(solution)/shard_map/psum | solution.py:59
  1725.4 0.9 fusion.22
  1726.3 214.4 %all-reduce.4 = bf16[32,2048]{1,0:T(8,128)(2,1)S(1)} all-reduce(f32[32,2048]{1,0:T(8,128)S(1)} %fusion.22), channel_id=1, replica_groups=mesh['row'=64,'col'=4] {'row'}, use_global_device_ids=true, to_apply=%region_6.7 | all-reduce | flops 65536 | bytes 393216 | tf_op jit(solution)/shard_map/psum | solution.py:62
  1940.7 1.7 fusion.30
  1942.5 87.3 %all_gather.12 = bf16[32,2048]{0,1:T(8,128)(2,1)} all-gather(bf16[32,32]{0,1:T(8,128)(2,1)S(1)} %copy.32), channel_id=1, replica_groups=mesh['row'=64,'col'=4] {'row'}, dimensions={1}, use_global_device_ids=true | all-gather | bytes 133120 | tf_op jit(solution)/shard_map/all_gather | solution.py:65
  2029.8 2.3 gather_fusion
  2032.1 0.9 fusion.4
  2033.1 47.8 %all_gather.13 = bf16[32,2048]{0,1:T(8,128)(2,1)S(1)} all-gather(bf16[32,32]{0,1:T(8,128)(2,1)S(1)} %copy.33), channel_id=1, replica_groups=mesh['row'=64,'col'=4] {'row'}, dimensions={1}, use_global_device_ids=true | all-gather | bytes 133120 | tf_op jit(solution)/shard_map/all_gather | solution.py:70
  2080.9 1.8 fusion.31
  2082.8 128.3 %all_gather.14 = bf16[32,8192]{0,1:T(8,128)(2,1)} all-gather(bf16[32,32]{0,1:T(8,128)(2,1)S(1)} %copy.34), channel_id=1, replica_groups=mesh['row'=64,'col'=4] {'row','col'}, dimensions={1}, use_global_device_ids=true | all-gather | bytes 526336 | tf_op jit(solution)/shard_map/all_gather | solution.py:72
  2211.1 9.5 gather_fusion.1
  2220.6 1.5 fusion.3
  2222.1 12.4 all_gather.15
  2234.4 1.4 fusion.33
  (56 shorter events, 5.8 us)
Async XLA Ops:
  7.2 1.6 copy-start
  7.2 3.8 copy-start.11
  7.2 3.8 copy-start.14
  7.2 3.9 copy-start.15
  7.2 30.7 %copy-start.1 = (bf16[4,256,512]{2,1,0:T(8,128)(2,1)S(1)}, bf16[4,256,512]{2,1,0:T(8,128)(2,1)}, u32[]{:S(2)}) copy-start(bf16[4,256,512]{2,1,0:T(8,128)(2,1)} %param.14) | copy-start | bytes 3145732
  7.2 30.7 %reduce-scatter.6.cloned.1.call-start = ((), (), s32[]{:S(2)}) async-start(), calls=%async_computation.3 | async-start | bytes 655360 | tf_op jit(solution)/shard_map/reduce_scatter | solution.py:40
  10.9 1164.2 %reduce-scatter.8.cloned.1.call-start = ((), (), s32[]{:S(2)}) async-start(), calls=%async_computation.4 | async-start | bytes 4210688 | tf_op jit(solution)/shard_map/reduce_scatter | solution.py:51
  11.2 26.7 %copy-start.9 = (pred[4,256]{1,0:T(4,128)(4,1)}, pred[4,256]{1,0:T(4,128)(4,1)S(1)}, u32[]{:S(2)}) copy-start(pred[4,256]{1,0:T(4,128)(4,1)S(1)} %broadcast_compare_fusion) | copy-start | bytes 3076
  11.2 43.2 %copy-start.7 = (s32[2048,1]{0,1:T(1,128)}, s32[2048,1]{0,1:T(1,128)S(1)}, u32[]{:S(2)}) copy-start(s32[2048,1]{0,1:T(1,128)S(1)} %compare_select_fusion) | copy-start | bytes 24580
  54.4 0.7 copy-start.12
  54.4 1120.7 %copy-start.4 = (bf16[1,32,2048]{2,1,0:T(8,128)(2,1)S(1)}, bf16[1,32,2048]{2,1,0:T(8,128)(2,1)}, u32[]{:S(2)}) copy-start(bf16[1,32,2048]{2,1,0:T(8,128)(2,1)} %param.19) | copy-start | bytes 393220
  54.4 1410.4 %copy-start.5 = (bf16[1,32,512]{2,1,0:T(8,128)(2,1)S(1)}, bf16[1,32,512]{2,1,0:T(8,128)(2,1)}, u32[]{:S(2)}) copy-start(bf16[1,32,512]{2,1,0:T(8,128)(2,1)} %param.20) | copy-start | bytes 98308
  54.4 1409.6 %reduce-scatter.10.cloned.1.call-start = ((), (), s32[]{:S(2)}) async-start(), calls=%async_computation.6 | async-start | bytes 1064960
  1177.2 292.3 %copy-start.8 = (s32[2048,1]{0,1:T(1,128)S(1)}, s32[2048,1]{0,1:T(1,128)}, u32[]{:S(2)}) copy-start(s32[2048,1]{0,1:T(1,128)} %copy-done.7) | copy-start | bytes 24580
  1177.2 292.9 %copy-start.13 = (bf16[32,32]{1,0:T(8,128)(2,1)S(1)}, bf16[32,32]{1,0:T(8,128)(2,1)}, u32[]{:S(2)}) copy-start(bf16[32,32]{1,0:T(8,128)(2,1)} %param.22) | copy-start | bytes 6148
  1177.2 548.2 %copy-start.3 = (bf16[32,2048]{1,0:T(8,128)(2,1)S(1)}, bf16[32,2048]{1,0:T(8,128)(2,1)}, u32[]{:S(2)}) copy-start(bf16[32,2048]{1,0:T(8,128)(2,1)} %param.23) | copy-start | bytes 393220
  1177.2 548.2 %all-reduce.3.cloned.1.call-start = ((), (), s32[]{:S(2)}) async-start(), calls=%async_computation.5 | async-start | bytes 2097152 | tf_op jit(solution)/shard_map/psum | solution.py:59
  1942.5 268.6 %copy-start.6 = (s32[2048]{0:T(1024)S(1)}, s32[2048]{0:T(1024)}, u32[]{:S(2)}) copy-start(s32[2048]{0:T(1024)} %broadcast_clamp_fusion) | copy-start | bytes 24580
  2080.9 139.7 %copy-start.2 = (f32[4,32,256]{2,1,0:T(8,128)S(1)}, f32[4,32,256]{2,1,0:T(8,128)}, u32[]{:S(2)}) copy-start(f32[4,32,256]{2,1,0:T(8,128)} %reduce-scatter.6.cloned.1.call-done) | copy-start | bytes 393220
  2080.9 139.7 %copy-start.10 = (pred[4,256]{1,0:T(4,128)(4,1)S(1)}, pred[4,256]{1,0:T(4,128)(4,1)}, u32[]{:S(2)}) copy-start(pred[4,256]{1,0:T(4,128)(4,1)} %copy-done.9) | copy-start | bytes 3076
Sparse Core Ops, SparseCore 0:
  11.0 26.8 reduce-scatter.5
  54.5 1120.5 reduce-scatter.7
  1179.6 284.3 reduce-scatter.9
  1470.2 255.1 all-reduce.2
where the time goes:
time: 2240 us
  waiting for transfers between devices  1690 us (75%)
  blocking collectives  490 us (22%)
    reduce_scatter x1, waiting for transfers between devices, body(): lax.psum_scatter(spread, ('row', 'col'), scatter_dimension=1, tiled=True)  1120 us
    unnamed x5, waiting for transfers between devices  286 us
    psum x1, waiting for transfers between devices, body(): root_total = lax.psum(root_term, ('row', 'col'))  254 us
    psum x1, blocking collectives, body(): lax.psum(jnp.dot(root_hb, root_inv, preferred_element_type=jnp.float32),...  214 us
    all_gather x1, blocking collectives, body(): lax.all_gather(mid_x.astype(jnp.bfloat16), ('row', 'col'), axis=1, tiled=...  128 us
    all_gather x1, blocking collectives, body(): lax.all_gather(root_x.astype(jnp.bfloat16), 'row', axis=1, tiled=True)  87.3 us
    all_gather x1, blocking collectives, body(): full_w = lax.all_gather(mid_wb, 'row', axis=1, tiled=True)  47.8 us
  transfers between devices with their start and end apart: 4, of which 4 were waited for; matrix products, arithmetic and copies ran while one was open for 0% of the time, Pallas kernels for 0%

commit v1 on v0

--- a/solution.py
+++ b/solution.py
@@ -62,7 +62,12 @@
     root_y = lax.psum(jnp.dot(root_hb, root_inv, preferred_element_type=jnp.float32), "row")
     root_yb = root_y.astype(jnp.bfloat16)
     root_x = jnp.einsum("kq,pq->kp", root_yb, root_inv, preferred_element_type=jnp.float32)
-    root_all = lax.all_gather(root_x.astype(jnp.bfloat16), "row", axis=1, tiled=True)
+    root_all = jnp.concatenate(
+        lax.all_to_all(
+            jnp.stack([root_x.astype(jnp.bfloat16)] * lax.axis_size("row")), "row", 0, 0
+        ),
+        axis=1,
+    )
     coupled = root_all[:, root_cols]
     mid_wb = (
         mid_y - jnp.einsum("kc,bc->kb", coupled, cpl_block, preferred_element_type=jnp.float32)

time: 2240 us -> 2210 us (0.987)
  blocking collectives: 490 us -> 402 us
  starting transfers between devices: 0.16 us -> 40.2 us
    all_gather x1 -> x0, blocking collectives: 87.3 us -> none  [body(): lax.all_gather(root_x.astype(jnp.bfloat16), 'row', axis=1, tiled=True)]
    all_to_all x0 -> x1, starting transfers between devices: none -> 40 us  [body(): lax.all_to_all(jnp.stack([root_x.astype(jnp.bfloat16)] * lax.axis_size('r...]
  transfers between devices with their start and end apart: 4 -> 5, of which waited for: 4 -> 5; matrix products, arithmetic and copies ran while one was open for 0% -> 0% of each run, Pallas kernels for 0% -> 0%
where the time goes in v1:
time: 2210 us
  waiting for transfers between devices  1700 us (77%)
  blocking collectives  402 us (18%)
  starting transfers between devices  40.2 us (2%)
    reduce_scatter x1, waiting for transfers between devices, body(): lax.psum_scatter(spread, ('row', 'col'), scatter_dimension=1, tiled=True)  1120 us
    unnamed x5, waiting for transfers between devices  287 us
    psum x1, waiting for transfers between devices, body(): root_total = lax.psum(root_term, ('row', 'col'))  255 us
    psum x1, blocking collectives, body(): lax.psum(jnp.dot(root_hb, root_inv, preferred_element_type=jnp.float32),...  214 us
    all_gather x1, blocking collectives, body(): lax.all_gather(mid_x.astype(jnp.bfloat16), ('row', 'col'), axis=1, tiled=...  127 us
    all_gather x1, blocking collectives, body(): full_w = lax.all_gather(mid_wb, 'row', axis=1, tiled=True)  48.3 us
  transfers between devices with their start and end apart: 5, of which 5 were waited for; matrix products, arithmetic and copies ran while one was open for 0% of the time, Pallas kernels for 0%

profile of v1, /device:TPU:8, one launch (start us, length us, event | category | flops | bytes accessed | tf_op | source)
XLA Modules:
  0.0 2207.2 jit_solution(6582327914194167996)
XLA Ops:
  7.3 1.5 copy-done
  8.8 2.1 fusion.32
  11.2 26.7 %reduce-scatter.6.cloned.1.call-done = f32[4,32,256]{2,1,0:T(8,128)} async-done(((f32[4,32,1024]{2,1,0:T(8,128)}), f32[4,32,256]{2,1,0:T(8,128)}) %reduce-scatter.6.cloned.1.call-update) | async-done | bytes 131088 | tf_op jit(solution)/shard_map/reduce_scatter | solution.py:40
  37.9 1.2 convolution_bitcast_fusion.1
  39.1 1.3 copy.29
  40.4 14.0 scatter_custom_fusion
  55.2 1120.5 %reduce-scatter.8.cloned.1.call-done = f32[32,32]{0,1:T(8,128)} async-done(((f32[32,8192]{0,1:T(8,128)}), f32[32,32]{0,1:T(8,128)}) %reduce-scatter.8.cloned.1.call-update) | async-done | bytes 4112 | tf_op jit(solution)/shard_map/reduce_scatter | solution.py:51
  1175.7 2.0 convolution_bitcast_fusion
  1178.5 286.4 %reduce-scatter.10.cloned.1.call-done = f32[32,32]{1,0:T(8,128)} async-done(((f32[2048,32]{1,0:T(8,128)}), f32[32,32]{1,0:T(8,128)}) %reduce-scatter.10.cloned.1.call-update) | async-done | bytes 4112
  1466.7 3.6 scatter_custom_fusion.1
  1471.1 255.1 %all-reduce.3.cloned.1.call-done = f32[32,2048]{0,1:T(8,128)} async-done(((f32[32,2048]{0,1:T(8,128)}), f32[32,2048]{0,1:T(8,128)}) %all-reduce.3.cloned.1.call-update) | async-done | bytes 262160 | tf_op jit(solution)/shard_map/psum | solution.py:59
  1727.1 214.4 %all-reduce.4 = bf16[32,2048]{1,0:T(8,128)(2,1)S(1)} all-reduce(f32[32,2048]{1,0:T(8,128)S(1)} %fusion.22), channel_id=1, replica_groups=mesh['row'=64,'col'=4] {'row'}, use_global_device_ids=true, to_apply=%region_6.7 | all-reduce | flops 65536 | bytes 393216 | tf_op jit(solution)/shard_map/psum | solution.py:62
  1941.5 1.7 fusion.30
  1944.2 2.1 reshape.153
  1946.3 40.0 %all-to-all-start = ((bf16[64,2,512]{2,1,0:T(2,128)(2,1)}), bf16[64,2,512]{2,1,0:T(2,128)(2,1)S(1)}, u32[]{:S(2)}, u32[]{:S(2)}) async-start(bf16[64,2,512]{2,1,0:T(2,128)(2,1)} %reshape.153), calls=%async_computation.2 | async-start | bytes 262144 | tf_op jit(solution)/shard_map/all_to_all | solution.py:66
  1987.8 8.0 all-to-all-done
  1995.8 1.1 reshape.154
  1996.9 2.2 gather_fusion
  1999.3 48.3 %all_gather.9 = bf16[32,2048]{0,1:T(8,128)(2,1)S(1)} all-gather(bf16[32,32]{0,1:T(8,128)(2,1)S(1)} %copy.33), channel_id=1, replica_groups=mesh['row'=64,'col'=4] {'row'}, dimensions={1}, use_global_device_ids=true | all-gather | bytes 133120 | tf_op jit(solution)/shard_map/all_gather | solution.py:75
  2048.6 127.3 %all_gather.10 = bf16[32,8192]{0,1:T(8,128)(2,1)} all-gather(bf16[32,32]{0,1:T(8,128)(2,1)S(1)} %copy.34), channel_id=1, replica_groups=mesh['row'=64,'col'=4] {'row','col'}, dimensions={1}, use_global_device_ids=true | all-gather | bytes 526336 | tf_op jit(solution)/shard_map/all_gather | solution.py:77
  2175.9 9.5 gather_fusion.1
  2185.4 1.5 fusion.3
  2186.9 12.4 all_gather.11
  2199.3 1.4 fusion.33
  (62 shorter events, 8.9 us)
Async XLA Ops:
  7.2 1.6 copy-start
  7.2 3.8 copy-start.12
  7.2 3.8 copy-start.15
  7.2 3.9 copy-start.16
  7.2 30.7 %copy-start.1 = (bf16[4,256,512]{2,1,0:T(8,128)(2,1)S(1)}, bf16[4,256,512]{2,1,0:T(8,128)(2,1)}, u32[]{:S(2)}) copy-start(bf16[4,256,512]{2,1,0:T(8,128)(2,1)} %param.14) | copy-start | bytes 3145732
  7.2 30.7 %reduce-scatter.6.cloned.1.call-start = ((), (), s32[]{:S(2)}) async-start(), calls=%async_computation.4 | async-start | bytes 655360 | tf_op jit(solution)/shard_map/reduce_scatter | solution.py:40
  10.9 1164.8 %reduce-scatter.8.cloned.1.call-start = ((), (), s32[]{:S(2)}) async-start(), calls=%async_computation.5 | async-start | bytes 4210688 | tf_op jit(solution)/shard_map/reduce_scatter | solution.py:51
  11.2 26.7 %copy-start.9 = (pred[4,256]{1,0:T(4,128)(4,1)}, pred[4,256]{1,0:T(4,128)(4,1)S(1)}, u32[]{:S(2)}) copy-start(pred[4,256]{1,0:T(4,128)(4,1)S(1)} %broadcast_compare_fusion) | copy-start | bytes 3076
  11.2 43.2 %copy-start.8 = (s32[2048,1]{0,1:T(1,128)}, s32[2048,1]{0,1:T(1,128)S(1)}, u32[]{:S(2)}) copy-start(s32[2048,1]{0,1:T(1,128)S(1)} %compare_select_fusion) | copy-start | bytes 24580
  54.4 0.7 copy-start.13
  54.4 1121.3 %copy-start.4 = (bf16[1,32,2048]{2,1,0:T(8,128)(2,1)S(1)}, bf16[1,32,2048]{2,1,0:T(8,128)(2,1)}, u32[]{:S(2)}) copy-start(bf16[1,32,2048]{2,1,0:T(8,128)(2,1)} %param.19) | copy-start | bytes 393220
  54.4 1411.3 %copy-start.6 = (bf16[1,32,512]{2,1,0:T(8,128)(2,1)S(1)}, bf16[1,32,512]{2,1,0:T(8,128)(2,1)}, u32[]{:S(2)}) copy-start(bf16[1,32,512]{2,1,0:T(8,128)(2,1)} %param.20) | copy-start | bytes 98308
  54.5 1410.5 %reduce-scatter.10.cloned.1.call-start = ((), (), s32[]{:S(2)}) async-start(), calls=%async_computation.7 | async-start | bytes 1064960
  1177.7 292.7 %copy-start.14 = (bf16[32,32]{1,0:T(8,128)(2,1)S(1)}, bf16[32,32]{1,0:T(8,128)(2,1)}, u32[]{:S(2)}) copy-start(bf16[32,32]{1,0:T(8,128)(2,1)} %param.22) | copy-start | bytes 6148
  1177.7 548.5 %copy-start.3 = (bf16[32,2048]{1,0:T(8,128)(2,1)S(1)}, bf16[32,2048]{1,0:T(8,128)(2,1)}, u32[]{:S(2)}) copy-start(bf16[32,2048]{1,0:T(8,128)(2,1)} %param.23) | copy-start | bytes 393220
  1177.7 548.4 %all-reduce.3.cloned.1.call-start = ((), (), s32[]{:S(2)}) async-start(), calls=%async_computation.6 | async-start | bytes 2097152 | tf_op jit(solution)/shard_map/psum | solution.py:59
  1178.5 292.6 %copy-start.11 = (s32[512,1]{0,1:T(1,128)}, s32[512,1]{0,1:T(1,128)S(1)}, u32[]{:S(2)}) copy-start(s32[512,1]{0,1:T(1,128)S(1)} %compare_select_fusion.1) | copy-start | bytes 6148
  1941.5 106.1 %copy-start.5 = (bf16[1,32,2048]{2,1,0:T(8,128)(2,1)S(1)}, bf16[1,32,2048]{2,1,0:T(8,128)(2,1)}, u32[]{:S(2)}) copy-start(bf16[1,32,2048]{2,1,0:T(8,128)(2,1)} %param.19) | copy-start | bytes 393220
  1943.2 55.8 %copy-start.7 = (bf16[1,32,512]{2,1,0:T(8,128)(2,1)S(1)}, bf16[1,32,512]{2,1,0:T(8,128)(2,1)}, u32[]{:S(2)}) copy-start(bf16[1,32,512]{2,1,0:T(8,128)(2,1)} %param.20) | copy-start | bytes 98308
  1946.3 49.5 %all-to-all-start = ((bf16[64,2,512]{2,1,0:T(2,128)(2,1)}), bf16[64,2,512]{2,1,0:T(2,128)(2,1)S(1)}, u32[]{:S(2)}, u32[]{:S(2)}) async-start(bf16[64,2,512]{2,1,0:T(2,128)(2,1)} %reshape.153), calls=%async_computation.2 | async-start | bytes 262144 | tf_op jit(solution)/shard_map/all_to_all | solution.py:66
  2047.6 137.8 %copy-start.2 = (f32[4,32,256]{2,1,0:T(8,128)S(1)}, f32[4,32,256]{2,1,0:T(8,128)}, u32[]{:S(2)}) copy-start(f32[4,32,256]{2,1,0:T(8,128)} %reduce-scatter.6.cloned.1.call-done) | copy-start | bytes 393220
  2047.6 137.8 %copy-start.10 = (pred[4,256]{1,0:T(4,128)(4,1)S(1)}, pred[4,256]{1,0:T(4,128)(4,1)}, u32[]{:S(2)}) copy-start(pred[4,256]{1,0:T(4,128)(4,1)} %copy-done.9) | copy-start | bytes 3076
Sparse Core Ops, SparseCore 0:
  11.0 26.8 reduce-scatter.5
  54.6 1121.0 reduce-scatter.7
  1180.2 284.7 reduce-scatter.9
  1471.1 254.9 all-reduce.2
